TPU v7x, 32 devices: a whole 2x2x4 slice. The times are simulated.
32 devices in a mesh: dp: 2 (over y), expert: 4 (over x, core), tensor: 4 (over z).
Axes of the slice: x: 2, y: 2, z: 4, core: 2. Of those that a mesh axis runs over, the one named last changes fastest.
Arguments:
- hidden_states: bfloat16 [256, 4096], P(('dp', 'expert'), 'tensor'), may hold values from -6 to 6
- chosen_experts: int32 [256, 2], P(('dp', 'expert')), may hold values from 0 to 3, all different within a row; in each aligned block of 32 rows (0 to 31, 32 to 63, ...) at most 16 rows name the same one
- choice_weights: float32 [256, 2], P(('dp', 'expert')), may hold values from 0.2 to 1
- gate_proj: bfloat16 [4, 4096, 8192], P('expert', None, ('dp', 'tensor')), may hold values from -0.09375 to 0.09375
- up_proj: bfloat16 [4, 4096, 8192], P('expert', None, ('dp', 'tensor')), may hold values from -0.09375 to 0.09375
- down_proj: bfloat16 [4, 8192, 4096], P('expert', 'dp', 'tensor'), may hold values from -0.0625 to 0.0625
Outputs:
- moe_output: bfloat16 [256, 4096], P(('dp', 'expert'), 'tensor')
Inputs may be any that keep to these rules, and one draw needn't show every extreme that they name: `chosen_experts`: each row names 2 different experts; among the 32 rows of one device no expert is named more than 16 times, a bound that some block reaches.
All inputs are finite; a program needn't handle non-finite values.
Results may differ from a plain program's by a relative error of at most 0.0058.
Values may be sent and summed in bfloat16 or wider, within the bound.
A program may use at most 64 MiB of HBM per device.

v0:
```python
import jax
import jax.numpy as jnp
from jax import lax
from jax.sharding import PartitionSpec as P

CAP = 16


def slot_tables(chosen_experts, experts, capacity):
    flat_ids = chosen_experts.reshape(-1)
    onehot = (flat_ids[:, None] == jnp.arange(experts, dtype=jnp.int32)[None, :]).astype(jnp.int32)
    before = jnp.cumsum(onehot, axis=0) - onehot
    position = jnp.sum(before * onehot, axis=1)
    return (flat_ids * capacity + position).reshape(chosen_experts.shape)


def body(hidden_states, chosen_experts, choice_weights, gate_proj, up_proj, down_proj):
    experts = lax.axis_size("expert")
    token_count = hidden_states.shape[0]
    feat_width = hidden_states.shape[1]
    slot_count = experts * CAP
    target = slot_tables(chosen_experts, experts, CAP)
    slot_ids = jnp.arange(slot_count, dtype=jnp.int32)
    placing = jnp.zeros((slot_count, token_count), jnp.float32)
    weights_table = jnp.zeros((token_count, slot_count), jnp.float32)
    for column in range(target.shape[1]):
        placing = placing + (slot_ids[:, None] == target[None, :, column]).astype(jnp.float32)
        weights_table = weights_table + jnp.where(
            target[:, column][:, None] == slot_ids[None, :],
            choice_weights[:, column][:, None],
            jnp.float32(0.0),
        )
    packed = jnp.dot(
        placing.astype(jnp.bfloat16), hidden_states, preferred_element_type=jnp.float32
    )
    packed = packed.astype(jnp.bfloat16).reshape(experts, CAP, feat_width)
    arrived = lax.all_to_all(packed, "expert", split_axis=0, concat_axis=0, tiled=True).reshape(
        slot_count, feat_width
    )
    gate_weights = gate_proj[0]
    up_weights = up_proj[0]
    down_weights = down_proj[0]
    features = lax.all_gather(arrived, "tensor", axis=1, tiled=True)
    shards = lax.all_gather(features, "dp", axis=0, tiled=True)
    gate_part = jnp.dot(shards, gate_weights, preferred_element_type=jnp.float32)
    up_part = jnp.dot(shards, up_weights, preferred_element_type=jnp.float32)
    activated = (jax.nn.silu(gate_part) * up_part).astype(jnp.bfloat16)
    unit_rows = lax.all_gather(activated, "tensor", axis=1, tiled=True)
    summed = lax.psum_scatter(
        jnp.dot(unit_rows, down_weights, preferred_element_type=jnp.float32),
        "dp",
        scatter_dimension=0,
        tiled=True,
    )
    outgoing = summed.astype(jnp.bfloat16).reshape(experts, CAP, feat_width)
    returned = lax.all_to_all(outgoing, "expert", split_axis=0, concat_axis=0, tiled=True).reshape(
        slot_count, feat_width
    )
    combined = jnp.dot(
        weights_table,
        returned.astype(jnp.float32),
        precision=lax.Precision.HIGHEST,
        preferred_element_type=jnp.float32,
    )
    return combined.astype(jnp.bfloat16)


def solution(mesh):
    in_specs = (
        P(("dp", "expert"), "tensor"),
        P(("dp", "expert"), None),
        P(("dp", "expert"), None),
        P("expert", None, ("dp", "tensor")),
        P("expert", None, ("dp", "tensor")),
        P("expert", "dp", "tensor"),
    )
    out_specs = P(("dp", "expert"), "tensor")
    return jax.shard_map(body, mesh=mesh, in_specs=in_specs, out_specs=out_specs, check_vma=False)
```

profile of v0, /device:TPU:0, one launch (start us, length us, event | category | flops | bytes accessed | tf_op | source)
XLA Modules:
  0.0 131.8 jit_solution(14651087666373031079)
XLA Ops:
  6.5 0.0 copy-start
  6.5 0.0 all-gather.3.cloned.1.call-start
  6.5 0.8 copy.13
  7.3 0.1 eq.71
  7.4 0.1 fusion.12
  7.5 0.1 reduce_window_sum.11
  7.6 0.2 select_reduce_fusion
  7.8 0.1 reduce_sum.12
  7.9 0.1 copy.14
  8.0 0.7 multiply_add_fusion
  8.7 0.0 copy-done
  8.7 0.2 convolution_convert_fusion
  8.9 8.6 %all_to_all.10 = bf16[4,16,1024]{2,1,0:T(8,128)(2,1)S(1)} all-to-all(bf16[4,16,1024]{2,1,0:T(8,128)(2,1)S(1)} %bitcast.31), channel_id=1, replica_groups=mesh['dp'=2,'expert'=4,'tensor'=4] {'expert'}, dimensions={0} | all-to-all | bytes 262144 | tf_op jit(solution)/shard_map/all_to_all | solution.py:37
  17.5 16.2 %all_gather.9 = bf16[64,4096]{1,0:T(8,128)(2,1)} all-gather(bf16[64,1024]{1,0:T(8,128)(2,1)S(1)} %bitcast.30), channel_id=1, replica_groups=mesh['dp'=2,'expert'=4,'tensor'=4] {'tensor'}, dimensions={1}, use_global_device_ids=true | all-gather | bytes 655360 | tf_op jit(solution)/shard_map/all_gather | solution.py:43
  33.8 0.0 all-gather.3.cloned.1.call-update
  33.8 0.0 all-gather.5.cloned.1.call-start
  33.8 22.4 %all-gather.3.cloned.1.call-done = bf16[128,4096]{1,0:T(8,128)(2,1)} async-done(((bf16[64,4096]{1,0:T(8,128)(2,1)}), bf16[128,4096]{1,0:T(8,128)(2,1)}) %all-gather.3.cloned.1.call-update) | async-done | bytes 1048592 | tf_op jit(solution)/shard_map/all_gather | solution.py:44
  56.2 5.0 %fusion.4 = f32[128,1024]{1,0:T(8,128)S(1)} fusion(bf16[128,4096]{1,0:T(8,128)(2,1)} %all-gather.3.cloned.1.call-done, bf16[1,4096,1024]{2,1,0:T(8,128)(2,1)} %param.9), kind=kOutput, calls=%fused_computation.4 | convolution fusion | flops 1073741824 | bytes 9961472 | tf_op jit(solution)/shard_map/dot_general | solution.py:45
  61.2 0.0 copy-done.1
  61.2 5.5 %fusion.9 = bf16[128,1024]{1,0:T(8,128)(2,1)} fusion(bf16[128,4096]{1,0:T(8,128)(2,1)S(1)} %copy-done.1, bf16[1,4096,1024]{2,1,0:T(8,128)(2,1)} %param.10, f32[128,1024]{1,0:T(8,128)S(1)} %fusion.4), kind=kOutput, calls=%fused_computation.7 | convolution fusion | flops 1074528256 | bytes 10223616 | tf_op jit(solution)/shard_map/dot_general | solution.py:46
  66.7 0.0 all-gather.5.cloned.1.call-update
  66.8 0.0 copy-start.2
  66.8 0.0 reduce-scatter.2.cloned.1.call-start
  66.8 28.0 %all-gather.5.cloned.1.call-done = bf16[128,4096]{1,0:T(8,128)(2,1)} async-done(((bf16[128,1024]{1,0:T(8,128)(2,1)}), bf16[128,4096]{1,0:T(8,128)(2,1)}) %all-gather.5.cloned.1.call-update) | async-done | bytes 1048592 | tf_op jit(solution)/shard_map/all_gather | solution.py:48
  94.8 5.8 %fusion = f32[128,1024]{1,0:T(8,128)} fusion(bf16[128,4096]{1,0:T(8,128)(2,1)} %all-gather.5.cloned.1.call-done, bf16[1,4096,1024]{2,1,0:T(8,128)(2,1)} %param.11), kind=kOutput, calls=%fused_computation | convolution fusion | flops 1073741824 | bytes 9961472 | tf_op jit(solution)/shard_map/dot_general | solution.py:50
  100.6 0.0 reduce-scatter.2.cloned.1.call-update
  100.7 14.2 %reduce-scatter.2.cloned.1.call-done = f32[64,1024]{1,0:T(8,128)} async-done(((f32[128,1024]{1,0:T(8,128)}), f32[64,1024]{1,0:T(8,128)}) %reduce-scatter.2.cloned.1.call-update) | async-done | bytes 262160 | tf_op jit(solution)/shard_map/reduce_scatter | solution.py:49
  114.9 1.6 %convert_element_type.31 = bf16[64,1024]{1,0:T(8,128)(2,1)} convert(f32[64,1024]{1,0:T(8,128)} %reduce-scatter.2.cloned.1.call-done) | non-fusion elementwise | flops 65536 | bytes 393216 | tf_op jit(solution)/shard_map/convert_element_type | solution.py:55
  116.5 3.3 %all-to-all-start.1 = ((bf16[4,16,1024]{2,1,0:T(8,128)(2,1)}), bf16[4,16,1024]{2,1,0:T(8,128)(2,1)S(1)}, u32[]{:S(2)}, u32[]{:S(2)}) async-start(bf16[4,16,1024]{2,1,0:T(8,128)(2,1)} %bitcast.9), calls=%async_computation.2 | async-start | bytes 262144 | tf_op jit(solution)/shard_map/all_to_all | solution.py:56
  119.8 0.0 copy-done.2
  119.8 4.6 %all-to-all-done.1 = bf16[4,16,1024]{2,1,0:T(8,128)(2,1)S(1)} async-done(((bf16[4,16,1024]{2,1,0:T(8,128)(2,1)}), bf16[4,16,1024]{2,1,0:T(8,128)(2,1)S(1)}, u32[]{:S(2)}, u32[]{:S(2)}) %all-to-all-start.1) | async-done | bytes 131104 | tf_op jit(solution)/shard_map/all_to_all | solution.py:56
  124.4 0.9 convolution_convert_fusion.1
  (3 shorter events, 0.0 us)
Async XLA Ops:
  6.5 2.2 %copy-start = (bf16[32,1024]{1,0:T(8,128)(2,1)S(1)}, bf16[32,1024]{1,0:T(8,128)(2,1)}, u32[]{:S(2)}) copy-start(bf16[32,1024]{1,0:T(8,128)(2,1)} %param.6) | copy-start | bytes 196612
  6.5 49.7 %all-gather.3.cloned.1.call-start = ((), (), s32[]{:S(2)}) async-start(), calls=%async_computation.3 | async-start | bytes 1572864 | tf_op jit(solution)/shard_map/all_gather | solution.py:44
  33.8 61.1 %all-gather.5.cloned.1.call-start = ((), (), s32[]{:S(2)}) async-start(), calls=%async_computation.4 | async-start | bytes 1310720 | tf_op jit(solution)/shard_map/all_gather | solution.py:48
  56.2 5.0 %copy-start.1 = (bf16[128,4096]{1,0:T(8,128)(2,1)S(1)}, bf16[128,4096]{1,0:T(8,128)(2,1)}, u32[]{:S(2)}) copy-start(bf16[128,4096]{1,0:T(8,128)(2,1)} %all-gather.3.cloned.1.call-done) | copy-start | bytes 3145732
  66.8 53.1 %copy-start.2 = (f32[32,2]{0,1:T(2,128)S(1)}, f32[32,2]{0,1:T(2,128)}, u32[]{:S(2)}) copy-start(f32[32,2]{0,1:T(2,128)} %param.8) | copy-start | bytes 772
  66.8 48.1 %reduce-scatter.2.cloned.1.call-start = ((), (), s32[]{:S(2)}) async-start(), calls=%async_computation.5 | async-start | bytes 786432 | tf_op jit(solution)/shard_map/reduce_scatter | solution.py:49
  116.5 7.9 %all-to-all-start.1 = ((bf16[4,16,1024]{2,1,0:T(8,128)(2,1)}), bf16[4,16,1024]{2,1,0:T(8,128)(2,1)S(1)}, u32[]{:S(2)}, u32[]{:S(2)}) async-start(bf16[4,16,1024]{2,1,0:T(8,128)(2,1)} %bitcast.9), calls=%async_computation.2 | async-start | bytes 262144 | tf_op jit(solution)/shard_map/all_to_all | solution.py:56
Sparse Core Ops, SparseCore 0:
  33.9 22.2 all-gather.2
  66.9 27.9 all-gather.4
  100.8 14.0 reduce-scatter.1
where the time goes:
time: 132 us
  waiting for transfers between devices  69.2 us (52%)
  blocking collectives  24.9 us (19%)
  matrix products  17.4 us (13%)
  between operations  13.2 us (10%)
  starting transfers between devices  3.41 us (3%)
  other arithmetic  2.66 us (2%)
    all_gather x1, waiting for transfers between devices, body(): unit_rows = lax.all_gather(activated, 'tensor', axis=1, tiled=True)  28 us
    all_gather x1, waiting for transfers between devices, body(): shards = lax.all_gather(features, 'dp', axis=0, tiled=True)  22.4 us
    all_gather x1, blocking collectives, body(): features = lax.all_gather(arrived, 'tensor', axis=1, tiled=True)  16.2 us
    reduce_scatter x1, waiting for transfers between devices, body(): lax.psum_scatter(jnp.dot(unit_rows, down_weights, preferred_element_type=...  14.2 us
    all_to_all x1, blocking collectives, body(): lax.all_to_all(packed, 'expert', split_axis=0, concat_axis=0, tiled=True)  8.64 us
    dot_general x1, matrix products, body(): jnp.dot(unit_rows, down_weights, preferred_element_type=jnp.float32)  5.79 us
    dot_general x1, matrix products, body(): up_part = jnp.dot(shards, up_weights, preferred_element_type=jnp.float32)  5.48 us
    dot_general x1, matrix products, body(): jnp.dot(shards, gate_weights, preferred_element_type=jnp.float32)  5.03 us
  transfers between devices with their start and end apart: 4, of which 4 were waited for; matrix products, arithmetic and copies ran while one was open for 0% of the time, Pallas kernels for 0%

commit v1 on v0

--- a/solution.py
+++ b/solution.py
@@ -4,6 +4,24 @@
 from jax.sharding import PartitionSpec as P
 
 CAP = 16
+
+
+def collect(shard, axis, dim):
+    ways, here, step = (lax.axis_size(axis), lax.axis_index(axis), shard.shape[dim])
+    shape = [n * ways if d == dim else n for d, n in enumerate(shard.shape)]
+    full = lax.dynamic_update_slice_in_dim(
+        jnp.zeros(shape, shard.dtype), shard, here * step, axis=dim
+    )
+    going_up = going_down = shard
+    for far in range(1, ways // 2 + 1):
+        going_up = lax.ppermute(going_up, axis, [(d, (d + 1) % ways) for d in range(ways)])
+        full = lax.dynamic_update_slice_in_dim(full, going_up, (here - far) % ways * step, axis=dim)
+        if 2 * far < ways:
+            going_down = lax.ppermute(going_down, axis, [(d, (d - 1) % ways) for d in range(ways)])
+            full = lax.dynamic_update_slice_in_dim(
+                full, going_down, (here + far) % ways * step, axis=dim
+            )
+    return full
 
 
 def slot_tables(chosen_experts, experts, capacity):
@@ -40,7 +58,7 @@
     gate_weights = gate_proj[0]
     up_weights = up_proj[0]
     down_weights = down_proj[0]
-    features = lax.all_gather(arrived, "tensor", axis=1, tiled=True)
+    features = collect(arrived, "tensor", 1)
     shards = lax.all_gather(features, "dp", axis=0, tiled=True)
     gate_part = jnp.dot(shards, gate_weights, preferred_element_type=jnp.float32)
     up_part = jnp.dot(shards, up_weights, preferred_element_type=jnp.float32)

time: 132 us -> 129 us (0.977)
  blocking collectives: 24.9 us -> 8.64 us
  waiting for transfers between devices: 69.2 us -> 77.4 us
  starting transfers between devices: 3.41 us -> 7.23 us
    all_gather x1 -> x0, blocking collectives: 16.2 us -> none  [body(): features = lax.all_gather(arrived, 'tensor', axis=1, tiled=True)]
    ppermute x0 -> x3, waiting for transfers between devices: none -> 11 us  [the longest x2 10.2 us: collect(): lax.ppermute(going_up, axis, [(d, (d + 1) % ways) for d in range(ways)])]
    ppermute x0 -> x3, starting transfers between devices: none -> 3.83 us  [the longest x1 2.25 us: collect(): lax.ppermute(going_down, axis, [(d, (d - 1) % ways) for d in range(ways)])]
    all_gather x1, waiting for transfers between devices: 22.4 us -> 19.6 us  [body(): shards = lax.all_gather(features, 'dp', axis=0, tiled=True)]
  transfers between devices with their start and end apart: 4 -> 7, of which waited for: 4 -> 7; matrix products, arithmetic and copies ran while one was open for 0% -> 0% of each run, Pallas kernels for 0% -> 0%
where the time goes in v1:
time: 129 us
  waiting for transfers between devices  77.4 us (60%)
  matrix products  17.4 us (13%)
  between operations  13.2 us (10%)
  blocking collectives  8.64 us (7%)
  starting transfers between devices  7.23 us (6%)
  other arithmetic  2.66 us (2%)
  local copies, waits for them, and re-layouts  2 us (2%)
    all_gather x1, waiting for transfers between devices, body(): unit_rows = lax.all_gather(activated, 'tensor', axis=1, tiled=True)  28 us
    all_gather x1, waiting for transfers between devices, body(): shards = lax.all_gather(features, 'dp', axis=0, tiled=True)  19.6 us
    reduce_scatter x1, waiting for transfers between devices, body(): lax.psum_scatter(jnp.dot(unit_rows, down_weights, preferred_element_type=...  14.2 us
    ppermute x2, waiting for transfers between devices, collect(): lax.ppermute(going_up, axis, [(d, (d + 1) % ways) for d in range(ways)])  10.2 us
    all_to_all x1, blocking collectives, body(): lax.all_to_all(packed, 'expert', split_axis=0, concat_axis=0, tiled=True)  8.64 us
    dot_general x1, matrix products, body(): jnp.dot(unit_rows, down_weights, preferred_element_type=jnp.float32)  5.79 us
    dot_general x1, matrix products, body(): up_part = jnp.dot(shards, up_weights, preferred_element_type=jnp.float32)  5.49 us
    dot_general x1, matrix products, body(): jnp.dot(shards, gate_weights, preferred_element_type=jnp.float32)  5.03 us
  transfers between devices with their start and end apart: 7, of which 7 were waited for; matrix products, arithmetic and copies ran while one was open for 0% of the time, Pallas kernels for 0%

profile of v1, /device:TPU:0, one launch (start us, length us, event | category | flops | bytes accessed | tf_op | source)
XLA Modules:
  0.0 128.6 jit_solution(5760717315470923389)
XLA Ops:
  6.5 0.8 copy.13
  7.3 0.1 eq.75
  7.4 0.1 fusion.6
  7.5 0.1 reduce_window_sum.11
  7.6 0.2 select_reduce_fusion
  7.8 0.1 reduce_sum.12
  7.9 0.1 copy.14
  8.0 0.7 multiply_add_fusion
  8.7 0.2 convolution_convert_fusion
  8.9 8.6 %all_to_all.10 = bf16[4,16,1024]{2,1,0:T(8,128)(2,1)S(1)} all-to-all(bf16[4,16,1024]{2,1,0:T(8,128)(2,1)S(1)} %bitcast.31), channel_id=1, replica_groups=mesh['dp'=2,'expert'=4,'tensor'=4] {'expert'}, dimensions={0} | all-to-all | bytes 262144 | tf_op jit(solution)/shard_map/all_to_all | solution.py:55
  17.5 1.6 %collective-permute-start = (bf16[64,1024]{1,0:T(8,128)(2,1)S(1)}, bf16[64,1024]{1,0:T(8,128)(2,1)S(1)}, u32[]{:S(2)}, u32[]{:S(2)}) collective-permute-start(bf16[64,1024]{1,0:T(8,128)(2,1)S(1)} %bitcast.28), channel_id=1, source_target_pairs={{0,1},{1,2},{2,3},{3,0},{4,5},{5,6},{6,7},{7,4},{8,9},{9,10},{10,1... | collective-permute-start | bytes 393224 | tf_op jit(solution)/shard_map/ppermute | solution.py:17
  19.1 2.2 %collective-permute-start.1 = (bf16[64,1024]{1,0:T(8,128)(2,1)S(1)}, bf16[64,1024]{1,0:T(8,128)(2,1)S(1)}, u32[]{:S(2)}, u32[]{:S(2)}) collective-permute-start(bf16[64,1024]{1,0:T(8,128)(2,1)S(1)} %bitcast.29), channel_id=1, source_target_pairs={{0,3},{1,0},{2,1},{3,2},{4,7},{5,4},{6,5},{7,6},{8,11},{9,8},{10,9... | collective-permute-start | bytes 393224 | tf_op jit(solution)/shard_map/ppermute | solution.py:20
  21.4 4.3 %collective-permute-done = bf16[64,1024]{1,0:T(8,128)(2,1)S(1)} collective-permute-done((bf16[64,1024]{1,0:T(8,128)(2,1)S(1)}, bf16[64,1024]{1,0:T(8,128)(2,1)S(1)}, u32[]{:S(2)}, u32[]{:S(2)}) %collective-permute-start) | collective-permute-done | bytes 131104 | tf_op jit(solution)/shard_map/ppermute | solution.py:17
  25.7 0.8 collective-permute-done.1
  26.5 5.9 %collective-permute-done.2 = bf16[64,1024]{1,0:T(8,128)(2,1)S(1)} collective-permute-done((bf16[64,1024]{1,0:T(8,128)(2,1)S(1)}, bf16[64,1024]{1,0:T(8,128)(2,1)S(1)}, u32[]{:S(2)}, u32[]{:S(2)}) %collective-permute-start.2) | collective-permute-done | bytes 131104 | tf_op jit(solution)/shard_map/ppermute | solution.py:17
  32.5 0.8 copy-done.2
  33.3 0.0 all-gather.3.cloned.1.call-update
  33.3 0.0 all-gather.5.cloned.1.call-start
  33.3 19.6 %all-gather.3.cloned.1.call-done = bf16[128,4096]{1,0:T(8,128)(2,1)} async-done(((bf16[64,4096]{1,0:T(8,128)(2,1)}), bf16[128,4096]{1,0:T(8,128)(2,1)}) %all-gather.3.cloned.1.call-update) | async-done | bytes 1048592 | tf_op jit(solution)/shard_map/all_gather | solution.py:62
  52.9 5.0 %fusion.4 = f32[128,1024]{1,0:T(8,128)S(1)} fusion(bf16[128,4096]{1,0:T(8,128)(2,1)} %all-gather.3.cloned.1.call-done, bf16[1,4096,1024]{2,1,0:T(8,128)(2,1)} %param.9), kind=kOutput, calls=%fused_computation.4 | convolution fusion | flops 1073741824 | bytes 9961472 | tf_op jit(solution)/shard_map/dot_general | solution.py:63
  58.0 5.5 %multiply_convert_fusion = bf16[128,1024]{1,0:T(8,128)(2,1)} fusion(f32[128,1024]{1,0:T(8,128)S(1)} %fusion.4, bf16[128,4096]{1,0:T(8,128)(2,1)S(1)} %copy-done.1, bf16[1,4096,1024]{2,1,0:T(8,128)(2,1)} %param.10), kind=kOutput, calls=%fused_computation.8 | convolution fusion | flops 1074528256 | bytes 10223616 | tf_op jit(solution)/shard_map/dot_general | solution.py:64
  63.5 0.0 all-gather.5.cloned.1.call-update
  63.5 0.0 copy-start.3
  63.5 0.0 reduce-scatter.2.cloned.1.call-start
  63.6 28.0 %all-gather.5.cloned.1.call-done = bf16[128,4096]{1,0:T(8,128)(2,1)} async-done(((bf16[128,1024]{1,0:T(8,128)(2,1)}), bf16[128,4096]{1,0:T(8,128)(2,1)}) %all-gather.5.cloned.1.call-update) | async-done | bytes 1048592 | tf_op jit(solution)/shard_map/all_gather | solution.py:66
  91.6 5.8 %fusion = f32[128,1024]{1,0:T(8,128)} fusion(bf16[128,4096]{1,0:T(8,128)(2,1)} %all-gather.5.cloned.1.call-done, bf16[1,4096,1024]{2,1,0:T(8,128)(2,1)} %param.11), kind=kOutput, calls=%fused_computation | convolution fusion | flops 1073741824 | bytes 9961472 | tf_op jit(solution)/shard_map/dot_general | solution.py:68
  97.4 0.0 reduce-scatter.2.cloned.1.call-update
  97.4 14.2 %reduce-scatter.2.cloned.1.call-done = f32[64,1024]{1,0:T(8,128)} async-done(((f32[128,1024]{1,0:T(8,128)}), f32[64,1024]{1,0:T(8,128)}) %reduce-scatter.2.cloned.1.call-update) | async-done | bytes 262160 | tf_op jit(solution)/shard_map/reduce_scatter | solution.py:67
  111.6 1.6 %convert_element_type.31 = bf16[64,1024]{1,0:T(8,128)(2,1)} convert(f32[64,1024]{1,0:T(8,128)} %reduce-scatter.2.cloned.1.call-done) | non-fusion elementwise | flops 65536 | bytes 393216 | tf_op jit(solution)/shard_map/convert_element_type | solution.py:73
  113.2 3.3 %all-to-all-start.1 = ((bf16[4,16,1024]{2,1,0:T(8,128)(2,1)}), bf16[4,16,1024]{2,1,0:T(8,128)(2,1)S(1)}, u32[]{:S(2)}, u32[]{:S(2)}) async-start(bf16[4,16,1024]{2,1,0:T(8,128)(2,1)} %bitcast.9), calls=%async_computation.2 | async-start | bytes 262144 | tf_op jit(solution)/shard_map/all_to_all | solution.py:74
  116.6 4.6 %all-to-all-done.1 = bf16[4,16,1024]{2,1,0:T(8,128)(2,1)S(1)} async-done(((bf16[4,16,1024]{2,1,0:T(8,128)(2,1)}), bf16[4,16,1024]{2,1,0:T(8,128)(2,1)S(1)}, u32[]{:S(2)}, u32[]{:S(2)}) %all-to-all-start.1) | async-done | bytes 131104 | tf_op jit(solution)/shard_map/all_to_all | solution.py:74
  121.1 0.9 convolution_convert_fusion.1
  (15 shorter events, 0.1 us)
Async XLA Ops:
  6.5 2.2 %copy-start = (bf16[32,1024]{1,0:T(8,128)(2,1)S(1)}, bf16[32,1024]{1,0:T(8,128)(2,1)}, u32[]{:S(2)}) copy-start(bf16[32,1024]{1,0:T(8,128)(2,1)} %param.6) | copy-start | bytes 196612
  6.5 46.4 %all-gather.3.cloned.1.call-start = ((), (), s32[]{:S(2)}) async-start(), calls=%async_computation.3 | async-start | bytes 1572864 | tf_op jit(solution)/shard_map/all_gather | solution.py:62
  17.5 8.2 %collective-permute-start = (bf16[64,1024]{1,0:T(8,128)(2,1)S(1)}, bf16[64,1024]{1,0:T(8,128)(2,1)S(1)}, u32[]{:S(2)}, u32[]{:S(2)}) collective-permute-start(bf16[64,1024]{1,0:T(8,128)(2,1)S(1)} %bitcast.28), channel_id=1, source_target_pairs={{0,1},{1,2},{2,3},{3,0},{4,5},{5,6},{6,7},{7,4},{8,9},{9,10},{10,1... | collective-permute-start | bytes 393224 | tf_op jit(solution)/shard_map/ppermute | solution.py:17
  19.1 7.4 %collective-permute-start.1 = (bf16[64,1024]{1,0:T(8,128)(2,1)S(1)}, bf16[64,1024]{1,0:T(8,128)(2,1)S(1)}, u32[]{:S(2)}, u32[]{:S(2)}) collective-permute-start(bf16[64,1024]{1,0:T(8,128)(2,1)S(1)} %bitcast.29), channel_id=1, source_target_pairs={{0,3},{1,0},{2,1},{3,2},{4,7},{5,4},{6,5},{7,6},{8,11},{9,8},{10,9... | collective-permute-start | bytes 393224 | tf_op jit(solution)/shard_map/ppermute | solution.py:20
  25.7 6.8 %collective-permute-start.2 = (bf16[64,1024]{1,0:T(8,128)(2,1)S(1)}, bf16[64,1024]{1,0:T(8,128)(2,1)S(1)}, u32[]{:S(2)}, u32[]{:S(2)}) collective-permute-start(bf16[64,1024]{1,0:T(8,128)(2,1)S(1)} %collective-permute-done), channel_id=1, source_target_pairs={{0,1},{1,2},{2,3},{3,0},{4,5},{5,6},{6,7},{7,4},{8,9},{9,10},{10,1... | collective-permute-start | bytes 393224 | tf_op jit(solution)/shard_map/ppermute | solution.py:17
  32.4 0.8 copy-start.2
  33.3 58.3 %all-gather.5.cloned.1.call-start = ((), (), s32[]{:S(2)}) async-start(), calls=%async_computation.4 | async-start | bytes 1310720 | tf_op jit(solution)/shard_map/all_gather | solution.py:66
  52.9 5.0 %copy-start.1 = (bf16[128,4096]{1,0:T(8,128)(2,1)S(1)}, bf16[128,4096]{1,0:T(8,128)(2,1)}, u32[]{:S(2)}) copy-start(bf16[128,4096]{1,0:T(8,128)(2,1)} %all-gather.3.cloned.1.call-done) | copy-start | bytes 3145732
  63.5 53.1 %copy-start.3 = (f32[32,2]{0,1:T(2,128)S(1)}, f32[32,2]{0,1:T(2,128)}, u32[]{:S(2)}) copy-start(f32[32,2]{0,1:T(2,128)} %param.8) | copy-start | bytes 772
  63.5 48.1 %reduce-scatter.2.cloned.1.call-start = ((), (), s32[]{:S(2)}) async-start(), calls=%async_computation.5 | async-start | bytes 786432 | tf_op jit(solution)/shard_map/reduce_scatter | solution.py:67
  113.2 7.9 %all-to-all-start.1 = ((bf16[4,16,1024]{2,1,0:T(8,128)(2,1)}), bf16[4,16,1024]{2,1,0:T(8,128)(2,1)S(1)}, u32[]{:S(2)}, u32[]{:S(2)}) async-start(bf16[4,16,1024]{2,1,0:T(8,128)(2,1)} %bitcast.9), calls=%async_computation.2 | async-start | bytes 262144 | tf_op jit(solution)/shard_map/all_to_all | solution.py:74
Sparse Core Ops, SparseCore 0:
  33.4 19.4 all-gather.2
  63.6 27.9 all-gather.4
  97.5 14.0 reduce-scatter.1
